TPU v7x, 128 devices: a whole 4x4x4 slice. The times are simulated.
128 devices in a mesh: row: 16 (over y, z), col: 8 (over x, core).
Axes of the slice: x: 4, y: 4, z: 4, core: 2. Of those that a mesh axis runs over, the one named last changes fastest.
Arguments:
- blocks: bfloat16 [16, 8, 128, 4096], P('row', 'col'), may hold values from -0.25 to 0.25
- block_row: int32 [16, 8, 128], P('row', 'col'), may hold values from 0 to 15
- block_col: int32 [16, 8, 128], P('row', 'col'), may hold values from 0 to 31
- counts: int32 [16, 8], P('row', 'col'), may hold values from 0 to 128, as said below
- vectors: float32 [256, 4096], P(('col', 'row')), may hold values from -6 to 6
- row_mass: float32 [256, 64], P(('row', 'col')), may hold values from 0.25 to 4
- col_mass: float32 [256, 64], P(('col', 'row')), may hold values from 0.25 to 4
Outputs:
- subspace: float32 [256, 4096], P(('col', 'row'))
Inputs may be any that keep to these rules, and one draw needn't show every extreme that they name: `counts`: in every row panel one tile uses all 128 slots; every other tile uses at most 8.
All inputs are finite; a program needn't handle non-finite values.
Results may differ from a plain program's by a relative error of at most 0.0085.
Values may be sent and summed in bfloat16 or wider, within the bound.
A program may use at most 64 MiB of HBM per device.

v0:
```python
import jax
import jax.numpy as jnp
from jax import lax
from jax.sharding import PartitionSpec as P

ITERS = 4


def rotate(projected, gram):
    lower = jnp.linalg.cholesky(gram)
    inverse = lax.linalg.triangular_solve(
        lower, jnp.eye(gram.shape[0], dtype=jnp.float32), left_side=True, lower=True
    )
    return jnp.einsum(
        "kl,bli->bki",
        inverse,
        projected,
        precision=lax.Precision.HIGHEST,
        preferred_element_type=jnp.float32,
    )


def local_gram(projected):
    return jnp.einsum(
        "bki,bli->kl",
        projected,
        projected,
        precision=lax.Precision.HIGHEST,
        preferred_element_type=jnp.float32,
    )


def per_device(blocks, block_row, block_col, counts, vectors, row_mass, col_mass):
    tile = blocks[0, 0]
    n_cap = tile.shape[0]
    bsize = row_mass.shape[1]
    vecs = vectors.shape[1] // bsize
    own = vectors.shape[0]
    n_row = lax.axis_size("row")
    n_col = lax.axis_size("col")
    row_panel = own * n_col
    col_panel = own * n_row
    total_boxes = float(own * bsize * n_row * n_col)
    rows_idx = block_row[0, 0]
    cols_idx = block_col[0, 0]
    live = jnp.arange(n_cap) < counts[0, 0]
    fwd_ids = jnp.where(live, rows_idx, row_panel)
    bwd_ids = jnp.where(live, cols_idx, col_panel)
    square = tile.reshape(n_cap, bsize, bsize)
    col_mass_panel = lax.all_gather(col_mass, "row", axis=0, tiled=True)
    row_mass_panel = lax.all_gather(row_mass, "col", axis=0, tiled=True)
    inv_col = 1.0 / jnp.sqrt(col_mass_panel)
    current = lax.all_gather(vectors, "row", axis=0, tiled=True).reshape(col_panel, vecs, bsize)
    for step in range(ITERS):
        scaled = (current * inv_col[:, None, :]).astype(jnp.bfloat16)
        forward_taken = jnp.take(scaled, cols_idx, axis=0)
        forward_product = jnp.einsum(
            "bij,bkj->bki", square, forward_taken, preferred_element_type=jnp.float32
        )
        forward_summed = jax.ops.segment_sum(forward_product, fwd_ids, num_segments=row_panel + 1)
        rows_sum = lax.psum(forward_summed[:row_panel], "col")
        weighted = (rows_sum * row_mass_panel[:, None, :]).astype(jnp.bfloat16)
        taken = jnp.take(weighted, rows_idx, axis=0)
        product = jnp.einsum("bij,bki->bkj", square, taken, preferred_element_type=jnp.float32)
        summed = jax.ops.segment_sum(product, bwd_ids, num_segments=col_panel + 1)
        cols_sum = lax.psum(summed[:col_panel], "row")
        projected = cols_sum * inv_col[:, None, :]
        gram = lax.psum(local_gram(projected), "col") / total_boxes
        current = rotate(projected, gram)
    me = lax.axis_index("row")
    mine = lax.dynamic_slice_in_dim(current, me * own, own, 0)
    return mine.reshape(own, vecs * bsize)


def solution(mesh):
    in_specs = (
        P("row", "col", None, None),
        P("row", "col", None),
        P("row", "col", None),
        P("row", "col"),
        P(("col", "row"), None),
        P(("row", "col"), None),
        P(("col", "row"), None),
    )
    out_specs = P(("col", "row"), None)
    return jax.shard_map(
        per_device, mesh=mesh, in_specs=in_specs, out_specs=out_specs, check_vma=False
    )
```

profile of v0, /device:TPU:0, one launch (start us, length us, event | category | flops | bytes accessed | tf_op | source)
XLA Modules:
  0.0 997.5 jit_solution(7439342869983005372)
XLA Ops:
  7.9 24.9 %all-gather.1 = f32[16,2,64]{2,1,0:T(2,128)S(1)} all-gather(f32[1,2,64]{2,1,0:T(2,128)} %bitcast.111), channel_id=1, replica_groups=mesh['row'=16,'col'=8] {'row'}, dimensions={0}, use_global_device_ids=true | all-gather | bytes 8704 | tf_op jit(solution)/shard_map/all_gather | solution.py:50
  32.8 23.5 %all-gather = f32[16,2,4096]{2,1,0:T(2,128)S(1)} all-gather(f32[1,2,4096]{2,1,0:T(2,128)} %bitcast.110), channel_id=1, replica_groups=mesh['row'=16,'col'=8] {'row'}, dimensions={0}, use_global_device_ids=true | all-gather | bytes 557056 | tf_op jit(solution)/shard_map/all_gather | solution.py:53
  65.8 4.8 fusion.14
  70.6 13.5 %scatter_fusion = f32[17,64,64]{2,1,0:T(8,128)S(1)} fusion(f32[17,64,64]{2,1,0:T(8,128)S(1)} %broadcast.82.clone.2, s32[128]{0:T(128)S(1)} %get-tuple-element.8, f32[128,64,64]{2,1,0:T(8,128)} %fusion.14), kind=kCustom, calls=%fused_computation.8 | custom fusion | flops 524288 | bytes 6291968 | tf_op jit(solution)/shard_map/scatter-add | solution.py:60
  85.1 10.7 %all-gather.2 = f32[8,2,64]{2,1,0:T(2,128)S(1)} all-gather(f32[1,2,64]{2,1,0:T(2,128)S(1)} %bitcast.112), channel_id=1, replica_groups=mesh['row'=16,'col'=8] {'col'}, dimensions={0}, use_global_device_ids=true | all-gather | bytes 4608 | tf_op jit(solution)/shard_map/all_gather | solution.py:51
  95.8 48.5 %all-reduce.9.cloned.1.call-done = f32[16,64,64]{2,1,0:T(8,128)} async-done(((f32[16,64,64]{2,1,0:T(8,128)}), f32[16,64,64]{2,1,0:T(8,128)}) %all-reduce.9.cloned.1.call-update) | async-done | bytes 262160 | tf_op jit(solution)/shard_map/psum | solution.py:61
  152.0 13.5 %scatter_fusion.1 = f32[33,64,64]{2,1,0:T(8,128)S(1)} fusion(f32[33,64,64]{2,1,0:T(8,128)S(1)} %broadcast.81.clone.2, s32[128]{0:T(128)S(1)} %get-tuple-element.6, f32[128,64,64]{2,1,0:T(8,128)} %fusion.12), kind=kCustom, calls=%fused_computation.9 | custom fusion | flops 524288 | bytes 6291968 | tf_op jit(solution)/shard_map/scatter-add | solution.py:65
  166.7 86.6 %all-reduce.11.cloned.1.call-done = f32[32,64,64]{2,1,0:T(8,128)} async-done(((f32[32,64,64]{2,1,0:T(8,128)}), f32[32,64,64]{2,1,0:T(8,128)}) %all-reduce.11.cloned.1.call-update) | async-done | bytes 524304 | tf_op jit(solution)/shard_map/psum | solution.py:66
  256.0 24.8 %psum.86 = f32[64,64]{0,1:T(8,128)S(1)} all-reduce(f32[64,64]{0,1:T(8,128)S(1)} %convolution_bitcast_fusion.7), channel_id=1, replica_groups=mesh['row'=16,'col'=8] {'col'}, use_global_device_ids=true, to_apply=%region_4.7 | all-reduce | flops 4096 | bytes 32768 | tf_op jit(solution)/shard_map/psum | solution.py:68
  280.9 5.8 cholesky.74
  288.1 4.9 custom-call.8
  304.3 13.5 %scatter_fusion.2 = f32[17,64,64]{2,1,0:T(8,128)S(1)} fusion(f32[17,64,64]{2,1,0:T(8,128)S(1)} %broadcast.82.clone.1, s32[128]{0:T(128)S(1)} %get-tuple-element.8, f32[128,64,64]{2,1,0:T(8,128)} %fusion.10), kind=kCustom, calls=%fused_computation.10 | custom fusion | flops 524288 | bytes 6291968 | tf_op jit(solution)/shard_map/scatter-add | solution.py:60
  318.7 57.4 %all-reduce.13.cloned.1.call-done = f32[16,64,64]{2,1,0:T(8,128)} async-done(((f32[16,64,64]{2,1,0:T(8,128)}), f32[16,64,64]{2,1,0:T(8,128)}) %all-reduce.13.cloned.1.call-update) | async-done | bytes 262160 | tf_op jit(solution)/shard_map/psum | solution.py:61
  383.7 13.5 %scatter_fusion.3 = f32[33,64,64]{2,1,0:T(8,128)S(1)} fusion(f32[33,64,64]{2,1,0:T(8,128)S(1)} %broadcast.81.clone.1, s32[128]{0:T(128)S(1)} %get-tuple-element.6, f32[128,64,64]{2,1,0:T(8,128)} %fusion.8), kind=kCustom, calls=%fused_computation.11 | custom fusion | flops 524288 | bytes 6291968 | tf_op jit(solution)/shard_map/scatter-add | solution.py:65
  398.4 86.6 %all-reduce.15.cloned.1.call-done = f32[32,64,64]{2,1,0:T(8,128)} async-done(((f32[32,64,64]{2,1,0:T(8,128)}), f32[32,64,64]{2,1,0:T(8,128)}) %all-reduce.15.cloned.1.call-update) | async-done | bytes 524304 | tf_op jit(solution)/shard_map/psum | solution.py:66
  487.8 24.4 %psum.89 = f32[64,64]{0,1:T(8,128)S(1)} all-reduce(f32[64,64]{0,1:T(8,128)S(1)} %convolution_bitcast_fusion.5), channel_id=1, replica_groups=mesh['row'=16,'col'=8] {'col'}, use_global_device_ids=true, to_apply=%region_11.16 | all-reduce | flops 4096 | bytes 32768 | tf_op jit(solution)/shard_map/psum | solution.py:68
  512.3 5.8 cholesky.85
  519.5 4.9 custom-call.9
  535.8 13.5 %scatter_fusion.4 = f32[17,64,64]{2,1,0:T(8,128)S(1)} fusion(f32[17,64,64]{2,1,0:T(8,128)S(1)} %broadcast.82.clone, s32[128]{0:T(128)S(1)} %get-tuple-element.8, f32[128,64,64]{2,1,0:T(8,128)} %fusion.6), kind=kCustom, calls=%fused_computation.12 | custom fusion | flops 524288 | bytes 6291968 | tf_op jit(solution)/shard_map/scatter-add | solution.py:60
  550.2 57.4 %all-reduce.17.cloned.1.call-done = f32[16,64,64]{2,1,0:T(8,128)} async-done(((f32[16,64,64]{2,1,0:T(8,128)}), f32[16,64,64]{2,1,0:T(8,128)}) %all-reduce.17.cloned.1.call-update) | async-done | bytes 262160 | tf_op jit(solution)/shard_map/psum | solution.py:61
  615.2 13.5 %scatter_fusion.5 = f32[33,64,64]{2,1,0:T(8,128)S(1)} fusion(f32[33,64,64]{2,1,0:T(8,128)S(1)} %broadcast.81.clone, s32[128]{0:T(128)S(1)} %get-tuple-element.6, f32[128,64,64]{2,1,0:T(8,128)} %fusion.4), kind=kCustom, calls=%fused_computation.13 | custom fusion | flops 524288 | bytes 6291968 | tf_op jit(solution)/shard_map/scatter-add | solution.py:65
  629.9 86.6 %all-reduce.19.cloned.1.call-done = f32[32,64,64]{2,1,0:T(8,128)} async-done(((f32[32,64,64]{2,1,0:T(8,128)}), f32[32,64,64]{2,1,0:T(8,128)}) %all-reduce.19.cloned.1.call-update) | async-done | bytes 524304 | tf_op jit(solution)/shard_map/psum | solution.py:66
  719.3 24.5 %psum.92 = f32[64,64]{0,1:T(8,128)S(1)} all-reduce(f32[64,64]{0,1:T(8,128)S(1)} %convolution_bitcast_fusion.3), channel_id=1, replica_groups=mesh['row'=16,'col'=8] {'col'}, use_global_device_ids=true, to_apply=%region_16.21 | all-reduce | flops 4096 | bytes 32768 | tf_op jit(solution)/shard_map/psum | solution.py:68
  743.9 5.8 cholesky.96
  751.1 4.9 custom-call.10
  767.3 13.5 %scatter_fusion.6 = f32[17,64,64]{2,1,0:T(8,128)S(1)} fusion(f32[17,64,64]{2,1,0:T(8,128)S(1)} %broadcast.82, s32[128]{0:T(128)S(1)} %get-tuple-element.8, f32[128,64,64]{2,1,0:T(8,128)} %fusion.2), kind=kCustom, calls=%fused_computation.14 | custom fusion | flops 524288 | bytes 6291968 | tf_op jit(solution)/shard_map/scatter-add | solution.py:60
  781.7 57.4 %all-reduce.21.cloned.1.call-done = f32[16,64,64]{2,1,0:T(8,128)} async-done(((f32[16,64,64]{2,1,0:T(8,128)}), f32[16,64,64]{2,1,0:T(8,128)}) %all-reduce.21.cloned.1.call-update) | async-done | bytes 262160 | tf_op jit(solution)/shard_map/psum | solution.py:61
  846.7 13.5 %scatter_fusion.7 = f32[33,64,64]{2,1,0:T(8,128)S(1)} fusion(f32[33,64,64]{2,1,0:T(8,128)S(1)} %broadcast.81, s32[128]{0:T(128)S(1)} %get-tuple-element.6, f32[128,64,64]{2,1,0:T(8,128)} %fusion), kind=kCustom, calls=%fused_computation.15 | custom fusion | flops 524288 | bytes 6291968 | tf_op jit(solution)/shard_map/scatter-add | solution.py:65
  861.4 86.7 %all-reduce.23.cloned.1.call-done = f32[32,64,64]{2,1,0:T(8,128)} async-done(((f32[32,64,64]{2,1,0:T(8,128)}), f32[32,64,64]{2,1,0:T(8,128)}) %all-reduce.23.cloned.1.call-update) | async-done | bytes 524304 | tf_op jit(solution)/shard_map/psum | solution.py:66
  950.8 24.5 %psum.95 = f32[64,64]{0,1:T(8,128)S(1)} all-reduce(f32[64,64]{0,1:T(8,128)S(1)} %convolution_bitcast_fusion.1), channel_id=1, replica_groups=mesh['row'=16,'col'=8] {'col'}, use_global_device_ids=true, to_apply=%region_21.26 | all-reduce | flops 4096 | bytes 32768 | tf_op jit(solution)/shard_map/psum | solution.py:68
  975.4 5.8 cholesky.107
  982.6 4.9 custom-call.11
  (121 shorter events, 102.5 us)
Async XLA Ops:
  6.5 51.4 %copy-start.4 = (bf16[1,1,128,4096]{3,2,1,0:T(8,128)(2,1)S(1)}, bf16[1,1,128,4096]{3,2,1,0:T(8,128)(2,1)}, u32[]{:S(2)}) copy-start(bf16[1,1,128,4096]{3,2,1,0:T(8,128)(2,1)} %param.14) | copy-start | bytes 3145732
  6.5 137.8 %all-reduce.9.cloned.1.call-start = ((), (), s32[]{:S(2)}) async-start(), calls=%async_computation | async-start | bytes 1048576 | tf_op jit(solution)/shard_map/psum | solution.py:61
  63.6 2.2 copy-start.6
  63.6 2.2 copy-start.7
  70.6 14.5 %copy-start.5 = (f32[2,64]{1,0:T(2,128)S(1)}, f32[2,64]{1,0:T(2,128)}, u32[]{:S(2)}) copy-start(f32[2,64]{1,0:T(2,128)} %param.19) | copy-start | bytes 1540
  85.0 168.2 %all-reduce.11.cloned.1.call-start = ((), (), s32[]{:S(2)}) async-start(), calls=%async_computation.1 | async-start | bytes 2097152 | tf_op jit(solution)/shard_map/psum | solution.py:66
  166.6 209.5 %all-reduce.13.cloned.1.call-start = ((), (), s32[]{:S(2)}) async-start(), calls=%async_computation.2 | async-start | bytes 1048576 | tf_op jit(solution)/shard_map/psum | solution.py:61
  253.2 40.0 %copy-start.1 = (f32[32,64,64]{2,1,0:T(8,128)S(1)}, f32[32,64,64]{2,1,0:T(8,128)}, u32[]{:S(2)}) copy-start(f32[32,64,64]{2,1,0:T(8,128)} %all-reduce.11.cloned.1.call-done) | copy-start | bytes 1572868
  318.7 166.4 %all-reduce.15.cloned.1.call-start = ((), (), s32[]{:S(2)}) async-start(), calls=%async_computation.3 | async-start | bytes 2097152 | tf_op jit(solution)/shard_map/psum | solution.py:66
  398.4 209.2 %all-reduce.17.cloned.1.call-start = ((), (), s32[]{:S(2)}) async-start(), calls=%async_computation.4 | async-start | bytes 1048576 | tf_op jit(solution)/shard_map/psum | solution.py:61
  485.1 39.6 %copy-start.2 = (f32[32,64,64]{2,1,0:T(8,128)S(1)}, f32[32,64,64]{2,1,0:T(8,128)}, u32[]{:S(2)}) copy-start(f32[32,64,64]{2,1,0:T(8,128)} %all-reduce.15.cloned.1.call-done) | copy-start | bytes 1572868
  550.1 166.4 %all-reduce.19.cloned.1.call-start = ((), (), s32[]{:S(2)}) async-start(), calls=%async_computation.5 | async-start | bytes 2097152 | tf_op jit(solution)/shard_map/psum | solution.py:66
  629.9 209.2 %all-reduce.21.cloned.1.call-start = ((), (), s32[]{:S(2)}) async-start(), calls=%async_computation.6 | async-start | bytes 1048576 | tf_op jit(solution)/shard_map/psum | solution.py:61
  716.6 39.7 %copy-start.3 = (f32[32,64,64]{2,1,0:T(8,128)S(1)}, f32[32,64,64]{2,1,0:T(8,128)}, u32[]{:S(2)}) copy-start(f32[32,64,64]{2,1,0:T(8,128)} %all-reduce.19.cloned.1.call-done) | copy-start | bytes 1572868
  781.7 166.4 %all-reduce.23.cloned.1.call-start = ((), (), s32[]{:S(2)}) async-start(), calls=%async_computation.7 | async-start | bytes 2097152 | tf_op jit(solution)/shard_map/psum | solution.py:66
  948.1 39.7 %copy-start = (f32[32,64,64]{2,1,0:T(8,128)S(1)}, f32[32,64,64]{2,1,0:T(8,128)}, u32[]{:S(2)}) copy-start(f32[32,64,64]{2,1,0:T(8,128)} %all-reduce.23.cloned.1.call-done) | copy-start | bytes 1572868
Sparse Core Ops, SparseCore 0:
  85.2 59.1 all-reduce.8
  166.7 86.4 all-reduce.10
  318.8 57.2 all-reduce.12
  398.5 86.4 all-reduce.14
  550.3 57.2 all-reduce.16
  630.0 86.5 all-reduce.18
  781.8 57.2 all-reduce.20
  861.6 86.4 all-reduce.22
where the time goes:
time: 1010 us; the launch traced here: 998 us
  waiting for transfers between devices  567 us (56%)
  other arithmetic  164 us (16%)
  blocking collectives  157 us (16%)
  matrix products  58.3 us (6%)
  local copies, waits for them, and re-layouts  36 us (4%)
  between operations  14.9 us (1%)
    psum x4, waiting for transfers between devices, per_device(): cols_sum = lax.psum(summed[:col_panel], 'row')  346 us
    psum x4, waiting for transfers between devices, per_device(): rows_sum = lax.psum(forward_summed[:row_panel], 'col')  221 us
    psum x4, blocking collectives, per_device(): gram = lax.psum(local_gram(projected), 'col') / total_boxes  98.2 us
    scatter-add x4, other arithmetic, per_device(): summed = jax.ops.segment_sum(product, bwd_ids, num_segments=col_panel + 1)  54.1 us
    scatter-add x4, other arithmetic, per_device(): jax.ops.segment_sum(forward_product, fwd_ids, num_segments=row_panel + 1)  54 us
    another operation x12, other arithmetic, rotate(): lower = jnp.linalg.cholesky(gram)  26.1 us
    all_gather x1, blocking collectives, per_device(): col_mass_panel = lax.all_gather(col_mass, 'row', axis=0, tiled=True)  24.9 us
    all_gather x1, blocking collectives, per_device(): lax.all_gather(vectors, 'row', axis=0, tiled=True)  23.5 us
  transfers between devices with their start and end apart: 8, of which 8 were waited for; matrix products, arithmetic and copies ran while one was open for 0% of the time, Pallas kernels for 0%

commit v1 on v0

--- a/solution.py
+++ b/solution.py
@@ -4,6 +4,11 @@
 from jax.sharding import PartitionSpec as P
 
 ITERS = 4
+
+
+def gather_and_add(x, mesh_axis):
+    shards = lax.all_gather(x, mesh_axis)
+    return jnp.sum(shards, axis=0)
 
 
 def rotate(projected, gram):
@@ -58,7 +63,7 @@
             "bij,bkj->bki", square, forward_taken, preferred_element_type=jnp.float32
         )
         forward_summed = jax.ops.segment_sum(forward_product, fwd_ids, num_segments=row_panel + 1)
-        rows_sum = lax.psum(forward_summed[:row_panel], "col")
+        rows_sum = gather_and_add(forward_summed[:row_panel], "col")
         weighted = (rows_sum * row_mass_panel[:, None, :]).astype(jnp.bfloat16)
         taken = jnp.take(weighted, rows_idx, axis=0)
         product = jnp.einsum("bij,bki->bkj", square, taken, preferred_element_type=jnp.float32)

time: 1010 us -> 904 us (0.90)
  waiting for transfers between devices: 567 us -> 456 us
    psum x4 -> x0, waiting for transfers between devices: 221 us -> none  [per_device(): rows_sum = lax.psum(forward_summed[:row_panel], 'col')]
    all_gather x0 -> x4, waiting for transfers between devices: none -> 106 us  [gather_and_add(): shards = lax.all_gather(x, mesh_axis)]
    reduce_sum x0 -> x4, other arithmetic: none -> 10.9 us  [gather_and_add(): return jnp.sum(shards, axis=0)]
where the time goes in v1:
time: 904 us; the launch traced here: 893 us
  waiting for transfers between devices  456 us (50%)
  other arithmetic  170 us (19%)
  blocking collectives  157 us (17%)
  matrix products  58.3 us (6%)
  local copies, waits for them, and re-layouts  35.9 us (4%)
  between operations  14.9 us (2%)
    psum x4, waiting for transfers between devices, per_device(): cols_sum = lax.psum(summed[:col_panel], 'row')  349 us
    all_gather x4, waiting for transfers between devices, gather_and_add(): shards = lax.all_gather(x, mesh_axis)  106 us
    psum x4, blocking collectives, per_device(): gram = lax.psum(local_gram(projected), 'col') / total_boxes  98.2 us
    scatter-add x4, other arithmetic, per_device(): summed = jax.ops.segment_sum(product, bwd_ids, num_segments=col_panel + 1)  54.1 us
    scatter-add x4, other arithmetic, per_device(): jax.ops.segment_sum(forward_product, fwd_ids, num_segments=row_panel + 1)  54 us
    another operation x12, other arithmetic, rotate(): lower = jnp.linalg.cholesky(gram)  26.1 us
    all_gather x1, blocking collectives, per_device(): col_mass_panel = lax.all_gather(col_mass, 'row', axis=0, tiled=True)  24.9 us
    all_gather x1, blocking collectives, per_device(): lax.all_gather(vectors, 'row', axis=0, tiled=True)  23.5 us
  transfers between devices with their start and end apart: 8, of which 8 were waited for; matrix products, arithmetic and copies ran while one was open for 0% of the time, Pallas kernels for 0%

profile of v1, /device:TPU:0, one launch (start us, length us, event | category | flops | bytes accessed | tf_op | source)
XLA Modules:
  0.0 893.0 jit_solution(1445277807393576746)
XLA Ops:
  7.9 24.9 %all-gather.5 = f32[16,2,64]{2,1,0:T(2,128)S(1)} all-gather(f32[1,2,64]{2,1,0:T(2,128)} %bitcast.119), channel_id=1, replica_groups=mesh['row'=16,'col'=8] {'row'}, dimensions={0}, use_global_device_ids=true | all-gather | bytes 8704 | tf_op jit(solution)/shard_map/all_gather | solution.py:55
  32.8 23.5 %all-gather.4 = f32[16,2,4096]{2,1,0:T(2,128)S(1)} all-gather(f32[1,2,4096]{2,1,0:T(2,128)} %bitcast.118), channel_id=1, replica_groups=mesh['row'=16,'col'=8] {'row'}, dimensions={0}, use_global_device_ids=true | all-gather | bytes 557056 | tf_op jit(solution)/shard_map/all_gather | solution.py:58
  65.8 4.8 fusion.14
  70.6 13.5 %scatter_fusion = f32[17,64,64]{2,1,0:T(8,128)S(1)} fusion(f32[17,64,64]{2,1,0:T(8,128)S(1)} %broadcast.82.clone.2, s32[128]{0:T(128)S(1)} %get-tuple-element.8, f32[128,64,64]{2,1,0:T(8,128)} %fusion.14), kind=kCustom, calls=%fused_computation.8 | custom fusion | flops 524288 | bytes 6291968 | tf_op jit(solution)/shard_map/scatter-add | solution.py:65
  85.1 10.7 %all-gather.6 = f32[8,2,64]{2,1,0:T(2,128)S(1)} all-gather(f32[1,2,64]{2,1,0:T(2,128)S(1)} %bitcast.120), channel_id=1, replica_groups=mesh['row'=16,'col'=8] {'col'}, dimensions={0}, use_global_device_ids=true | all-gather | bytes 4608 | tf_op jit(solution)/shard_map/all_gather | solution.py:56
  95.8 20.0 %all-gather.12.cloned.1.call-done = f32[128,64,64]{2,1,0:T(8,128)} async-done(((f32[16,64,64]{2,1,0:T(8,128)}), f32[128,64,64]{2,1,0:T(8,128)}) %all-gather.12.cloned.1.call-update) | async-done | bytes 2097168 | tf_op jit(solution)/shard_map/all_gather | solution.py:10
  125.1 13.5 %scatter_fusion.1 = f32[33,64,64]{2,1,0:T(8,128)S(1)} fusion(f32[33,64,64]{2,1,0:T(8,128)S(1)} %broadcast.81.clone.2, s32[128]{0:T(128)S(1)} %get-tuple-element.6, f32[128,64,64]{2,1,0:T(8,128)} %fusion.12), kind=kCustom, calls=%fused_computation.9 | custom fusion | flops 524288 | bytes 6291968 | tf_op jit(solution)/shard_map/scatter-add | solution.py:70
  139.8 87.4 %all-reduce.5.cloned.1.call-done = f32[32,64,64]{2,1,0:T(8,128)} async-done(((f32[32,64,64]{2,1,0:T(8,128)}), f32[32,64,64]{2,1,0:T(8,128)}) %all-reduce.5.cloned.1.call-update) | async-done | bytes 524304 | tf_op jit(solution)/shard_map/psum | solution.py:71
  229.9 24.8 %psum.57 = f32[64,64]{0,1:T(8,128)S(1)} all-reduce(f32[64,64]{0,1:T(8,128)S(1)} %convolution_bitcast_fusion.7), channel_id=1, replica_groups=mesh['row'=16,'col'=8] {'col'}, use_global_device_ids=true, to_apply=%region_4.7 | all-reduce | flops 4096 | bytes 32768 | tf_op jit(solution)/shard_map/psum | solution.py:73
  254.8 5.8 cholesky.74
  262.0 4.9 custom-call.8
  278.2 13.5 %scatter_fusion.2 = f32[17,64,64]{2,1,0:T(8,128)S(1)} fusion(f32[17,64,64]{2,1,0:T(8,128)S(1)} %broadcast.82.clone.1, s32[128]{0:T(128)S(1)} %get-tuple-element.8, f32[128,64,64]{2,1,0:T(8,128)} %fusion.10), kind=kCustom, calls=%fused_computation.10 | custom fusion | flops 524288 | bytes 6291968 | tf_op jit(solution)/shard_map/scatter-add | solution.py:65
  292.6 28.8 %all-gather.14.cloned.1.call-done = f32[128,64,64]{2,1,0:T(8,128)} async-done(((f32[16,64,64]{2,1,0:T(8,128)}), f32[128,64,64]{2,1,0:T(8,128)}) %all-gather.14.cloned.1.call-update) | async-done | bytes 2097168 | tf_op jit(solution)/shard_map/all_gather | solution.py:10
  330.8 13.5 %scatter_fusion.3 = f32[33,64,64]{2,1,0:T(8,128)S(1)} fusion(f32[33,64,64]{2,1,0:T(8,128)S(1)} %broadcast.81.clone.1, s32[128]{0:T(128)S(1)} %get-tuple-element.6, f32[128,64,64]{2,1,0:T(8,128)} %fusion.8), kind=kCustom, calls=%fused_computation.11 | custom fusion | flops 524288 | bytes 6291968 | tf_op jit(solution)/shard_map/scatter-add | solution.py:70
  345.5 87.3 %all-reduce.7.cloned.1.call-done = f32[32,64,64]{2,1,0:T(8,128)} async-done(((f32[32,64,64]{2,1,0:T(8,128)}), f32[32,64,64]{2,1,0:T(8,128)}) %all-reduce.7.cloned.1.call-update) | async-done | bytes 524304 | tf_op jit(solution)/shard_map/psum | solution.py:71
  435.6 24.4 %psum.59 = f32[64,64]{0,1:T(8,128)S(1)} all-reduce(f32[64,64]{0,1:T(8,128)S(1)} %convolution_bitcast_fusion.5), channel_id=1, replica_groups=mesh['row'=16,'col'=8] {'col'}, use_global_device_ids=true, to_apply=%region_11.16 | all-reduce | flops 4096 | bytes 32768 | tf_op jit(solution)/shard_map/psum | solution.py:73
  460.1 5.8 cholesky.85
  467.3 4.9 custom-call.9
  483.5 13.5 %scatter_fusion.4 = f32[17,64,64]{2,1,0:T(8,128)S(1)} fusion(f32[17,64,64]{2,1,0:T(8,128)S(1)} %broadcast.82.clone, s32[128]{0:T(128)S(1)} %get-tuple-element.8, f32[128,64,64]{2,1,0:T(8,128)} %fusion.6), kind=kCustom, calls=%fused_computation.12 | custom fusion | flops 524288 | bytes 6291968 | tf_op jit(solution)/shard_map/scatter-add | solution.py:65
  497.9 28.8 %all-gather.16.cloned.1.call-done = f32[128,64,64]{2,1,0:T(8,128)} async-done(((f32[16,64,64]{2,1,0:T(8,128)}), f32[128,64,64]{2,1,0:T(8,128)}) %all-gather.16.cloned.1.call-update) | async-done | bytes 2097168 | tf_op jit(solution)/shard_map/all_gather | solution.py:10
  536.1 13.5 %scatter_fusion.5 = f32[33,64,64]{2,1,0:T(8,128)S(1)} fusion(f32[33,64,64]{2,1,0:T(8,128)S(1)} %broadcast.81.clone, s32[128]{0:T(128)S(1)} %get-tuple-element.6, f32[128,64,64]{2,1,0:T(8,128)} %fusion.4), kind=kCustom, calls=%fused_computation.13 | custom fusion | flops 524288 | bytes 6291968 | tf_op jit(solution)/shard_map/scatter-add | solution.py:70
  550.8 87.4 %all-reduce.9.cloned.1.call-done = f32[32,64,64]{2,1,0:T(8,128)} async-done(((f32[32,64,64]{2,1,0:T(8,128)}), f32[32,64,64]{2,1,0:T(8,128)}) %all-reduce.9.cloned.1.call-update) | async-done | bytes 524304 | tf_op jit(solution)/shard_map/psum | solution.py:71
  640.9 24.5 %psum.61 = f32[64,64]{0,1:T(8,128)S(1)} all-reduce(f32[64,64]{0,1:T(8,128)S(1)} %convolution_bitcast_fusion.3), channel_id=1, replica_groups=mesh['row'=16,'col'=8] {'col'}, use_global_device_ids=true, to_apply=%region_16.21 | all-reduce | flops 4096 | bytes 32768 | tf_op jit(solution)/shard_map/psum | solution.py:73
  665.5 5.8 cholesky.96
  672.7 4.9 custom-call.10
  688.9 13.5 %scatter_fusion.6 = f32[17,64,64]{2,1,0:T(8,128)S(1)} fusion(f32[17,64,64]{2,1,0:T(8,128)S(1)} %broadcast.82, s32[128]{0:T(128)S(1)} %get-tuple-element.8, f32[128,64,64]{2,1,0:T(8,128)} %fusion.2), kind=kCustom, calls=%fused_computation.14 | custom fusion | flops 524288 | bytes 6291968 | tf_op jit(solution)/shard_map/scatter-add | solution.py:65
  703.3 28.8 %all-gather.18.cloned.1.call-done = f32[128,64,64]{2,1,0:T(8,128)} async-done(((f32[16,64,64]{2,1,0:T(8,128)}), f32[128,64,64]{2,1,0:T(8,128)}) %all-gather.18.cloned.1.call-update) | async-done | bytes 2097168 | tf_op jit(solution)/shard_map/all_gather | solution.py:10
  741.5 13.5 %scatter_fusion.7 = f32[33,64,64]{2,1,0:T(8,128)S(1)} fusion(f32[33,64,64]{2,1,0:T(8,128)S(1)} %broadcast.81, s32[128]{0:T(128)S(1)} %get-tuple-element.6, f32[128,64,64]{2,1,0:T(8,128)} %fusion), kind=kCustom, calls=%fused_computation.15 | custom fusion | flops 524288 | bytes 6291968 | tf_op jit(solution)/shard_map/scatter-add | solution.py:70
  756.2 87.4 %all-reduce.11.cloned.1.call-done = f32[32,64,64]{2,1,0:T(8,128)} async-done(((f32[32,64,64]{2,1,0:T(8,128)}), f32[32,64,64]{2,1,0:T(8,128)}) %all-reduce.11.cloned.1.call-update) | async-done | bytes 524304 | tf_op jit(solution)/shard_map/psum | solution.py:71
  846.3 24.5 %psum.63 = f32[64,64]{0,1:T(8,128)S(1)} all-reduce(f32[64,64]{0,1:T(8,128)S(1)} %convolution_bitcast_fusion.1), channel_id=1, replica_groups=mesh['row'=16,'col'=8] {'col'}, use_global_device_ids=true, to_apply=%region_21.26 | all-reduce | flops 4096 | bytes 32768 | tf_op jit(solution)/shard_map/psum | solution.py:73
  870.9 5.8 cholesky.107
  878.1 4.9 custom-call.11
  (125 shorter events, 109.1 us)
Async XLA Ops:
  6.5 51.4 %copy-start.4 = (bf16[1,1,128,4096]{3,2,1,0:T(8,128)(2,1)S(1)}, bf16[1,1,128,4096]{3,2,1,0:T(8,128)(2,1)}, u32[]{:S(2)}) copy-start(bf16[1,1,128,4096]{3,2,1,0:T(8,128)(2,1)} %param.14) | copy-start | bytes 3145732
  6.5 109.2 %all-gather.12.cloned.1.call-start = ((), (), s32[]{:S(2)}) async-start(), calls=%async_computation.4 | async-start | bytes 4718592 | tf_op jit(solution)/shard_map/all_gather | solution.py:10
  63.6 2.2 copy-start.6
  63.6 2.2 copy-start.7
  70.6 14.4 %copy-start.5 = (f32[2,64]{1,0:T(2,128)S(1)}, f32[2,64]{1,0:T(2,128)}, u32[]{:S(2)}) copy-start(f32[2,64]{1,0:T(2,128)} %param.19) | copy-start | bytes 1540
  85.0 142.1 %all-reduce.5.cloned.1.call-start = ((), (), s32[]{:S(2)}) async-start(), calls=%async_computation | async-start | bytes 2097152 | tf_op jit(solution)/shard_map/psum | solution.py:71
  139.8 181.7 %all-gather.14.cloned.1.call-start = ((), (), s32[]{:S(2)}) async-start(), calls=%async_computation.5 | async-start | bytes 4718592 | tf_op jit(solution)/shard_map/all_gather | solution.py:10
  227.2 40.0 %copy-start.1 = (f32[32,64,64]{2,1,0:T(8,128)S(1)}, f32[32,64,64]{2,1,0:T(8,128)}, u32[]{:S(2)}) copy-start(f32[32,64,64]{2,1,0:T(8,128)} %all-reduce.5.cloned.1.call-done) | copy-start | bytes 1572868
  292.6 140.2 %all-reduce.7.cloned.1.call-start = ((), (), s32[]{:S(2)}) async-start(), calls=%async_computation.1 | async-start | bytes 2097152 | tf_op jit(solution)/shard_map/psum | solution.py:71
  345.4 181.3 %all-gather.16.cloned.1.call-start = ((), (), s32[]{:S(2)}) async-start(), calls=%async_computation.6 | async-start | bytes 4718592 | tf_op jit(solution)/shard_map/all_gather | solution.py:10
  432.8 39.6 %copy-start.2 = (f32[32,64,64]{2,1,0:T(8,128)S(1)}, f32[32,64,64]{2,1,0:T(8,128)}, u32[]{:S(2)}) copy-start(f32[32,64,64]{2,1,0:T(8,128)} %all-reduce.7.cloned.1.call-done) | copy-start | bytes 1572868
  497.9 140.3 %all-reduce.9.cloned.1.call-start = ((), (), s32[]{:S(2)}) async-start(), calls=%async_computation.2 | async-start | bytes 2097152 | tf_op jit(solution)/shard_map/psum | solution.py:71
  550.7 181.4 %all-gather.18.cloned.1.call-start = ((), (), s32[]{:S(2)}) async-start(), calls=%async_computation.7 | async-start | bytes 4718592 | tf_op jit(solution)/shard_map/all_gather | solution.py:10
  638.2 39.7 %copy-start.3 = (f32[32,64,64]{2,1,0:T(8,128)S(1)}, f32[32,64,64]{2,1,0:T(8,128)}, u32[]{:S(2)}) copy-start(f32[32,64,64]{2,1,0:T(8,128)} %all-reduce.9.cloned.1.call-done) | copy-start | bytes 1572868
  703.3 140.3 %all-reduce.11.cloned.1.call-start = ((), (), s32[]{:S(2)}) async-start(), calls=%async_computation.3 | async-start | bytes 2097152 | tf_op jit(solution)/shard_map/psum | solution.py:71
  843.6 39.7 %copy-start = (f32[32,64,64]{2,1,0:T(8,128)S(1)}, f32[32,64,64]{2,1,0:T(8,128)}, u32[]{:S(2)}) copy-start(f32[32,64,64]{2,1,0:T(8,128)} %all-reduce.11.cloned.1.call-done) | copy-start | bytes 1572868
Sparse Core Ops, SparseCore 0:
  85.1 30.5 all-gather.11
  139.9 87.2 all-reduce.4
  292.7 28.6 all-gather.13
  345.6 87.2 all-reduce.6
  498.0 28.6 all-gather.15
  550.9 87.2 all-reduce.8
  703.4 28.6 all-gather.17
  756.3 87.2 all-reduce.10
